TPU v7x, 32 devices: a whole 2x2x4 slice. The times are simulated.
32 devices in a mesh: dp: 2 (over x), row: 4 (over y, core), col: 4 (over z).
Axes of the slice: x: 2, y: 2, z: 4, core: 2. Of those that a mesh axis runs over, the one named last changes fastest.
Arguments:
- inputs: bfloat16 [14568, 12, 128], P(('dp', 'row'), 'col'), may hold values from -15 to 15
- mixer_weight: float32 [768, 2304], P('row', 'col'), may hold values from -0.3125 to 0.3125
- mixer_bias: float32 [12, 128], P('col', 'row'), may hold values from -3 to 3
- merge_weight: float32 [768, 768], P(('col', 'row')), may hold values from -0.875 to 0.875
- merge_bias: float32 [12, 64], P('col', 'row'), may hold values from -3 to 3
- expand_weight: float32 [768, 3072], P('row', 'col'), may hold values from -0.21875 to 0.21875
- expand_bias: float32 [12, 256], P('col', 'row'), may hold values from -3 to 3
- reduce_weight: float32 [3072, 768], P(('col', 'row')), may hold values from -0.109375 to 0.109375
- reduce_bias: float32 [12, 64], P('col', 'row'), may hold values from -3 to 3
- first_gain: float32 [12, 64], P('col', 'row'), may hold values from 0.1 to 1.9
- first_shift: float32 [12, 64], P('col', 'row'), may hold values from -3 to 3
- second_gain: float32 [12, 64], P('col', 'row'), may hold values from 0.1 to 1.9
- second_shift: float32 [12, 64], P('col', 'row'), may hold values from -3 to 3
- cotangent: bfloat16 [14568, 12, 128], P(('dp', 'row'), 'col'), may hold values from -6 to 6
Outputs:
- outputs: bfloat16 [14568, 12, 128], P(('dp', 'row'), 'col')
- input_grad: float32 [14568, 12, 128], P(('dp', 'row'), 'col')
- grad_mixer_weight: float32 [768, 2304], P('row', 'col')
- grad_mixer_bias: float32 [12, 128], P('col', 'row')
- grad_merge_weight: float32 [768, 768], P(('col', 'row'))
- grad_merge_bias: float32 [12, 64], P('col', 'row')
- grad_expand_weight: float32 [768, 3072], P('row', 'col')
- grad_expand_bias: float32 [12, 256], P('col', 'row')
- grad_reduce_weight: float32 [3072, 768], P(('col', 'row'))
- grad_reduce_bias: float32 [12, 64], P('col', 'row')
- grad_first_gain: float32 [12, 64], P('col', 'row')
- grad_first_shift: float32 [12, 64], P('col', 'row')
- grad_second_gain: float32 [12, 64], P('col', 'row')
- grad_second_shift: float32 [12, 64], P('col', 'row')
All inputs are finite; a program needn't handle non-finite values.
Results may differ from a plain program's by a relative error of at most 0.012.
The roundings to bfloat16 on the way count: a program that leaves them out, or rounds other values in their place, can miss the bound.
Values may be sent and summed in bfloat16 or wider, within the bound.
A program may use at most 192 MiB of HBM per device.

v0:
```python
import jax
import jax.numpy as jnp
from jax import lax
from jax.sharding import PartitionSpec as P

D = 768
HD = 64
LEN = 1214
EPSILON = 1e-06


def to_rows(values):
    halves = values.shape[0]
    groups = values.shape[1]
    return (
        values.reshape(halves, groups, 2, HD).transpose(0, 2, 1, 3).reshape(2 * halves, groups * HD)
    )


def from_rows(values):
    halves = values.shape[0] // 2
    groups = values.shape[1] // HD
    return (
        values.reshape(halves, 2, groups, HD).transpose(0, 2, 1, 3).reshape(halves, groups, 2 * HD)
    )


def exact_gelu(values):
    return jax.nn.gelu(values, approximate=False)


def inner_rows(left, right):
    return lax.dot_general(
        left, right, (((0,), (0,)), ((), ())), preferred_element_type=jnp.float32
    )


def times_transposed(left, right):
    return lax.dot_general(
        left, right, (((1,), (1,)), ((), ())), preferred_element_type=jnp.float32
    )


def as_vector(values):
    return values.astype(jnp.float32).reshape(-1)


def row_sum(values):
    return lax.psum(values, "col")


def norm_shard(values, gain, shift):
    centre = row_sum(jnp.sum(values, axis=1)) / D
    centered = values - centre[:, None]
    spread = row_sum(jnp.sum(centered * centered, axis=1)) / D
    inverse = lax.rsqrt(spread + EPSILON)
    scaled = centered * inverse[:, None]
    return (scaled * gain + shift, scaled, inverse)


def spread_rows(values):
    return lax.all_gather(values, "col", axis=1, tiled=True)


def gather_grads(values):
    return lax.all_gather(values, "col", axis=1, tiled=True)


def norm_back(partial_rows, scaled, inverse, gain):
    shard = lax.psum_scatter(partial_rows, "col", scatter_dimension=1, tiled=True)
    grad_gain = jnp.sum(shard * scaled, axis=0)
    grad_shift = jnp.sum(shard, axis=0)
    upstream = shard * gain
    first_sum, second_sum = lax.psum(
        (jnp.sum(upstream, axis=1), jnp.sum(upstream * scaled, axis=1)), "col"
    )
    result = inverse[:, None] * (
        upstream - first_sum[:, None] / D - scaled * (second_sum[:, None] / D)
    )
    return (result, grad_gain, grad_shift)


def attend(parts):
    query, keyset, valueset = parts
    scores = times_transposed(query, keyset) * HD ** (-0.5)
    highest = jnp.max(scores, axis=1, keepdims=True)
    weights = jnp.exp(scores - highest)
    totals = jnp.sum(weights, axis=1, keepdims=True)
    chances = (weights / totals).astype(jnp.bfloat16)
    result = jnp.dot(chances, valueset, preferred_element_type=jnp.float32)
    return (result.astype(jnp.bfloat16), (highest + jnp.log(totals))[:, 0])


def attend_back(parts):
    query, keyset, valueset, upstream, logsum = parts
    scale = HD ** (-0.5)
    scores = times_transposed(query, keyset) * scale
    chances = jnp.exp(scores - logsum[:, None])
    grad_chances = times_transposed(upstream, valueset)
    grad_value = inner_rows(chances.astype(jnp.bfloat16), upstream)
    inner = jnp.sum(grad_chances * chances, axis=1, keepdims=True)
    grad_scores = (chances * (grad_chances - inner)).astype(jnp.bfloat16)
    grad_query = jnp.dot(grad_scores, keyset, preferred_element_type=jnp.float32) * scale
    grad_key = inner_rows(grad_scores, query) * scale
    return jnp.stack([grad_query, grad_key, grad_value], axis=1).astype(jnp.bfloat16)


def body(
    inputs,
    mixer_weight,
    mixer_bias,
    merge_weight,
    merge_bias,
    expand_weight,
    expand_bias,
    reduce_weight,
    reduce_bias,
    first_gain,
    first_shift,
    second_gain,
    second_shift,
    cotangent,
):
    (
        mixer_mat,
        mixer_vec,
        merge_mat,
        merge_vec,
        expand_mat,
        expand_vec,
        reduce_mat,
        reduce_vec,
        gain_one,
        shift_one,
        gain_two,
        shift_two,
    ) = (
        lax.all_gather(mixer_weight.astype(jnp.bfloat16), "row", axis=0, tiled=True),
        lax.all_gather(mixer_bias.astype(jnp.bfloat16), "row", axis=1, tiled=True),
        lax.all_gather(merge_weight.astype(jnp.bfloat16), "row", axis=0, tiled=True),
        lax.all_gather(merge_bias.astype(jnp.bfloat16), "row", axis=1, tiled=True),
        lax.all_gather(expand_weight.astype(jnp.bfloat16), "row", axis=0, tiled=True),
        lax.all_gather(expand_bias.astype(jnp.bfloat16), "row", axis=1, tiled=True),
        lax.all_gather(reduce_weight.astype(jnp.bfloat16), "row", axis=0, tiled=True),
        lax.all_gather(reduce_bias.astype(jnp.bfloat16), "row", axis=1, tiled=True),
        lax.all_gather(first_gain.astype(jnp.bfloat16), "row", axis=1, tiled=True),
        lax.all_gather(first_shift.astype(jnp.bfloat16), "row", axis=1, tiled=True),
        lax.all_gather(second_gain.astype(jnp.bfloat16), "row", axis=1, tiled=True),
        lax.all_gather(second_shift.astype(jnp.bfloat16), "row", axis=1, tiled=True),
    )
    rows = to_rows(inputs).astype(jnp.float32)
    cotan_rows = to_rows(cotangent)
    tokens = rows.shape[0]
    width = rows.shape[1]
    clips = tokens // LEN
    local_heads = width // HD
    hidden_width = expand_mat.shape[1]
    gain_first = as_vector(gain_one)
    gain_second = as_vector(gain_two)
    normed_one, scaled_one, inverse_one = norm_shard(rows, gain_first, as_vector(shift_one))
    full_one = spread_rows(normed_one.astype(jnp.bfloat16))
    pairs = mixer_vec.astype(jnp.float32).reshape(local_heads, 2, HD)
    full_bias = jnp.stack([pairs[:, 0], jnp.zeros_like(pairs[:, 0]), pairs[:, 1]], axis=1).reshape(
        -1
    )
    mixed = (jnp.dot(full_one, mixer_mat, preferred_element_type=jnp.float32) + full_bias).astype(
        jnp.bfloat16
    )
    blocks = (
        mixed.reshape(clips, LEN, local_heads, 3, HD)
        .transpose(3, 0, 2, 1, 4)
        .reshape(3, clips * local_heads, LEN, HD)
    )
    head_blocks, logsums = lax.map(attend, (blocks[0], blocks[1], blocks[2]))
    heads = (
        head_blocks.reshape(clips, local_heads, LEN, HD)
        .transpose(0, 2, 1, 3)
        .reshape(tokens, width)
    )
    branch = lax.psum_scatter(
        jnp.dot(heads, merge_mat, preferred_element_type=jnp.float32),
        "col",
        scatter_dimension=1,
        tiled=True,
    )
    state = rows + branch + as_vector(merge_vec)
    normed_two, scaled_two, inverse_two = norm_shard(state, gain_second, as_vector(shift_two))
    full_two = spread_rows(normed_two.astype(jnp.bfloat16))
    hidden = jnp.dot(full_two, expand_mat, preferred_element_type=jnp.float32) + as_vector(
        expand_vec
    )
    active = exact_gelu(hidden).astype(jnp.bfloat16)
    down = lax.psum_scatter(
        jnp.dot(active, reduce_mat, preferred_element_type=jnp.float32).astype(jnp.bfloat16),
        "col",
        scatter_dimension=1,
        tiled=True,
    ).astype(jnp.float32)
    outputs = from_rows((state + down + as_vector(reduce_vec)).astype(jnp.bfloat16))
    cotan_full = gather_grads(cotan_rows)
    grad_reduce_mat = inner_rows(active, cotan_full)
    grad_reduce_vec = jnp.sum(cotan_rows.astype(jnp.float32), axis=0)
    grad_active = times_transposed(cotan_full, reduce_mat)
    gelu_pull = jax.vjp(exact_gelu, hidden)[1]
    grad_hidden = gelu_pull(grad_active)[0].astype(jnp.bfloat16)
    grad_expand_mat = inner_rows(full_two, grad_hidden)
    grad_expand_vec = jnp.sum(grad_hidden.astype(jnp.float32), axis=0)
    back_two, grad_gain_two, grad_shift_two = norm_back(
        times_transposed(grad_hidden, expand_mat), scaled_two, inverse_two, gain_second
    )
    grad_state = cotan_rows.astype(jnp.float32) + back_two
    grad_branch = grad_state.astype(jnp.bfloat16)
    branch_full = gather_grads(grad_branch)
    grad_merge_mat = inner_rows(heads, branch_full)
    grad_merge_vec = jnp.sum(grad_branch.astype(jnp.float32), axis=0)
    grad_heads = times_transposed(branch_full, merge_mat).astype(jnp.bfloat16)
    grad_blocks = (
        grad_heads.reshape(clips, LEN, local_heads, HD)
        .transpose(0, 2, 1, 3)
        .reshape(clips * local_heads, LEN, HD)
    )
    mixed_grads = lax.map(attend_back, (blocks[0], blocks[1], blocks[2], grad_blocks, logsums))
    grad_mixed = (
        mixed_grads.reshape(clips, local_heads, LEN, 3, HD)
        .transpose(0, 2, 1, 3, 4)
        .reshape(tokens, 3 * width)
    )
    grad_mixer_mat = inner_rows(full_one, grad_mixed)
    bias_sums = jnp.sum(grad_mixed.astype(jnp.float32), axis=0).reshape(local_heads, 3, HD)
    grad_mixer_vec = jnp.stack([bias_sums[:, 0], bias_sums[:, 2]], axis=1).reshape(
        local_heads, 2 * HD
    )
    back_one, grad_gain_one, grad_shift_one = norm_back(
        times_transposed(grad_mixed, mixer_mat), scaled_one, inverse_one, gain_first
    )
    input_grad = from_rows(grad_state + back_one)
    (
        part_mixer_mat,
        part_mixer_vec,
        part_merge_mat,
        part_merge_vec,
        part_expand_mat,
        part_expand_vec,
        part_reduce_mat,
        part_reduce_vec,
        part_gain_one,
        part_shift_one,
        part_gain_two,
        part_shift_two,
    ) = (
        lax.psum_scatter(grad_mixer_mat, "row", scatter_dimension=0, tiled=True),
        lax.psum_scatter(grad_mixer_vec, "row", scatter_dimension=1, tiled=True),
        lax.psum_scatter(grad_merge_mat, "row", scatter_dimension=0, tiled=True),
        lax.psum_scatter(
            grad_merge_vec.reshape(local_heads, HD), "row", scatter_dimension=1, tiled=True
        ),
        lax.psum_scatter(grad_expand_mat, "row", scatter_dimension=0, tiled=True),
        lax.psum_scatter(
            grad_expand_vec.reshape(local_heads, hidden_width // local_heads),
            "row",
            scatter_dimension=1,
            tiled=True,
        ),
        lax.psum_scatter(grad_reduce_mat, "row", scatter_dimension=0, tiled=True),
        lax.psum_scatter(
            grad_reduce_vec.reshape(local_heads, HD), "row", scatter_dimension=1, tiled=True
        ),
        lax.psum_scatter(
            grad_gain_one.reshape(local_heads, HD), "row", scatter_dimension=1, tiled=True
        ),
        lax.psum_scatter(
            grad_shift_one.reshape(local_heads, HD), "row", scatter_dimension=1, tiled=True
        ),
        lax.psum_scatter(
            grad_gain_two.reshape(local_heads, HD), "row", scatter_dimension=1, tiled=True
        ),
        lax.psum_scatter(
            grad_shift_two.reshape(local_heads, HD), "row", scatter_dimension=1, tiled=True
        ),
    )
    summed = lax.psum(
        (
            part_mixer_mat,
            part_mixer_vec,
            part_merge_mat,
            part_merge_vec,
            part_expand_mat,
            part_expand_vec,
            part_reduce_mat,
            part_reduce_vec,
            part_gain_one,
            part_shift_one,
            part_gain_two,
            part_shift_two,
        ),
        "dp",
    )
    return (
        outputs,
        input_grad,
        summed[0],
        summed[1],
        summed[2],
        summed[3],
        summed[4],
        summed[5],
        summed[6],
        summed[7],
        summed[8],
        summed[9],
        summed[10],
        summed[11],
    )


def solution(mesh):
    in_specs = (
        P(("dp", "row"), "col", None),
        P("row", "col"),
        P("col", "row"),
        P(("col", "row"), None),
        P("col", "row"),
        P("row", "col"),
        P("col", "row"),
        P(("col", "row"), None),
        P("col", "row"),
        P("col", "row"),
        P("col", "row"),
        P("col", "row"),
        P("col", "row"),
        P(("dp", "row"), "col", None),
    )
    out_specs = (
        P(("dp", "row"), "col", None),
        P(("dp", "row"), "col", None),
        P("row", "col"),
        P("col", "row"),
        P(("col", "row"), None),
        P("col", "row"),
        P("row", "col"),
        P("col", "row"),
        P(("col", "row"), None),
        P("col", "row"),
        P("col", "row"),
        P("col", "row"),
        P("col", "row"),
        P("col", "row"),
    )
    return jax.shard_map(body, mesh=mesh, in_specs=in_specs, out_specs=out_specs, check_vma=False)
```

profile of v0, /device:TPU:0, one launch (start us, length us, event | category | flops | bytes accessed | tf_op | source)
XLA Modules:
  0.0 1910.4 jit_solution(16474213476146647296)
XLA Ops:
  9.4 6.0 all-gather.1
  15.6 5.4 all-gather
  26.0 19.2 %psum.140 = f32[3642]{0:T(1024)S(1)} all-reduce(f32[3642]{0:T(1024)S(1)} %reduce_sum.167), channel_id=1, replica_groups=mesh['dp'=2,'row'=4,'col'=4] {'col'}, use_global_device_ids=true, to_apply=%region_1.0 | all-reduce | flops 3642 | bytes 29136 | tf_op jit(solution)/shard_map/psum | solution.py:49
  47.6 15.6 psum.141
  63.2 7.0 copy.134
  70.2 9.2 reshape.237
  84.7 5.1 all-gather.2
  90.3 6.0 all_gather.53
  96.3 10.2 all_gather.51
  106.5 82.4 %all-gather.15.cloned.1.call-done = bf16[3642,768]{0,1:T(8,128)(2,1)} async-done(((bf16[3642,192]{0,1:T(8,128)(2,1)}), bf16[3642,768]{0,1:T(8,128)(2,1)}) %all-gather.15.cloned.1.call-update) | async-done | bytes 5594128 | tf_op jit(solution)/shard_map/all_gather | solution.py:62
  188.9 8.5 add_convert_fusion.1
  197.5 14.2 reshape.217
  211.7 5.4 fusion.59
  224.7 5.2 copy.171
  229.9 64.2 %while.22 = (s32[]{:T(128)}, bf16[9,1214,64]{1,2,0:T(8,128)(2,1)}, f32[9,1214]{1,0:T(8,128)}, bf16[9,1214,64]{2,1,0:T(8,128)(2,1)}, bf16[9,1214,64]{2,1,0:T(8,12...) while((s32[]{:T(128)}, bf16[9,1214,64]{1,2,0:T(8,128)(2,1)}, f32[9,1214]{1,0:T(8,128)}, ...), condition=%wide.region_7.8_spmd, body=%wide.region_4.7_spmd.sunk | while | flops 387684832 | bytes 18843696 | solution.py:174
  303.9 7.4 fusion.62
  313.3 5.1 all-gather.5
  318.5 5.1 all-gather.4
  323.8 5.1 all-gather.3
  329.1 173.6 %reduce-scatter.33.cloned.1.call-done = f32[3642,192]{0,1:T(8,128)} async-done(((f32[3642,768]{0,1:T(8,128)}), f32[3642,192]{0,1:T(8,128)}) %reduce-scatter.33.cloned.1.call-update) | async-done | bytes 2797072 | tf_op jit(solution)/shard_map/reduce_scatter | solution.py:180
  505.7 18.5 psum.142
  524.5 15.5 psum.143
  546.7 6.0 copy.158
  552.7 7.8 reshape.223
  564.4 5.1 all-gather.6
  569.6 76.5 %all-gather.17.cloned.1.call-done = bf16[3642,768]{0,1:T(8,128)(2,1)} async-done(((bf16[3642,192]{0,1:T(8,128)(2,1)}), bf16[3642,768]{0,1:T(8,128)(2,1)}) %all-gather.17.cloned.1.call-update) | async-done | bytes 5594128 | tf_op jit(solution)/shard_map/all_gather | solution.py:62
  646.1 11.6 fusion.63
  657.7 6.0 all-gather.21.cloned.1.call-done
  663.7 107.1 %all-gather.23.cloned.1.call-done = bf16[3642,768]{0,1:T(8,128)(2,1)} async-done(((bf16[3642,192]{0,1:T(8,128)(2,1)}), bf16[3642,768]{0,1:T(8,128)(2,1)}) %all-gather.23.cloned.1.call-update) | async-done | bytes 5594128 | tf_op jit(solution)/shard_map/all_gather | solution.py:66
  770.8 35.6 %convert_reduce_fusion.1 = (f32[768]{0:T(1024)S(1)}, bf16[3642,768]{1,0:T(8,128)(2,1)S(1)}, f32[3642,768]{1,0:T(8,128)}) fusion(f32[3642,768]{1,0:T(8,128)} %fusion.63, f32[768]{0:T(1024)S(1)} %reshape.245, bf16[3642,768]{0,1:T(8,128)(2,1)} %all-gather.23.cloned.1.call-done, bf16[768,768]{1,0:T(8,128)(2,1)} %all-gather.21.cloned.1.call-done), kind=kOutput, calls=%fused_computation.57 | convolution fusion | flops 4506056704 | bytes 34750464 | tf_op jit(solution)/shard_map/dot_general | solution.py:39
  808.7 7.5 fusion.64
  816.5 190.9 %reduce-scatter.37.cloned.1.call-done = f32[3642,192]{0,1:T(8,128)} async-done(((f32[3642,768]{0,1:T(8,128)}), f32[3642,192]{0,1:T(8,128)}) %reduce-scatter.37.cloned.1.call-update) | async-done | bytes 2797072 | tf_op jit(solution)/shard_map/reduce_scatter | solution.py:70
  1011.0 18.8 all-reduce.1
  1034.8 104.1 %all-gather.25.cloned.1.call-done = bf16[3642,768]{0,1:T(8,128)(2,1)} async-done(((bf16[3642,192]{0,1:T(8,128)(2,1)}), bf16[3642,768]{0,1:T(8,128)(2,1)}) %all-gather.25.cloned.1.call-update) | async-done | bytes 5594128 | tf_op jit(solution)/shard_map/all_gather | solution.py:66
  1150.2 102.2 %while.23 = (s32[]{:T(128)}, bf16[9,1214,3,64]{1,3,2,0:T(8,128)(2,1)}, bf16[9,1214,64]{2,1,0:T(8,128)(2,1)}, bf16[9,1214,64]{2,1,0:T(8,128)(2,1)}, f32[9,1214]{1...) while((s32[]{:T(128)}, ...), condition=%wide.region_21.22_spmd, body=%wide.region_19.21_spmd.sunk | while | flops 956805568 | bytes 48504736 | solution.py:222
  1252.4 8.6 copy.207
  1261.0 12.2 reshape.227
  1273.2 9.8 fusion.65
  1288.1 11.1 multiply_convert_fusion.1
  1300.1 8.2 convert_reduce_fusion
  1309.5 10.5 fusion.69
  1320.1 10.5 fusion.68
  1330.7 5.2 fusion.67
  1336.1 10.0 fusion.66
  1346.2 9.2 convolution_convert_fusion
  1355.5 118.8 %reduce-scatter.39.cloned.1.call-done = f32[3642,192]{0,1:T(8,128)} async-done(((f32[3642,768]{0,1:T(8,128)}), f32[3642,192]{0,1:T(8,128)}) %reduce-scatter.39.cloned.1.call-update) | async-done | bytes 2797072 | tf_op jit(solution)/shard_map/reduce_scatter | solution.py:70
  1479.7 5.1 all-gather.7
  1485.8 12.0 reduce-scatter.55.cloned.1.call-done
  1498.6 21.8 %reduce-scatter.53.cloned.1.call-done = f32[64,3]{1,0:T(8,128)} async-done(((f32[256,3]{1,0:T(8,128)}), f32[64,3]{1,0:T(8,128)}) %reduce-scatter.53.cloned.1.call-update) | async-done | bytes 784
  1521.1 21.1 %reduce-scatter.63.cloned.1.call-done = f32[16,3]{1,0:T(8,128)} async-done(((f32[64,3]{1,0:T(8,128)}), f32[16,3]{1,0:T(8,128)}) %reduce-scatter.63.cloned.1.call-update) | async-done | bytes 208
  1543.0 21.2 %reduce-scatter.61.cloned.1.call-done = f32[16,3]{1,0:T(8,128)} async-done(((f32[64,3]{1,0:T(8,128)}), f32[16,3]{1,0:T(8,128)}) %reduce-scatter.61.cloned.1.call-update) | async-done | bytes 208
  1565.0 21.8 %reduce-scatter.51.cloned.1.call-done = f32[16,3]{1,0:T(8,128)} async-done(((f32[64,3]{1,0:T(8,128)}), f32[16,3]{1,0:T(8,128)}) %reduce-scatter.51.cloned.1.call-update) | async-done | bytes 208
  1587.5 21.6 %reduce-scatter.49.cloned.1.call-done = f32[32,3]{1,0:T(8,128)} async-done(((f32[128,3]{1,0:T(8,128)}), f32[32,3]{1,0:T(8,128)}) %reduce-scatter.49.cloned.1.call-update) | async-done | bytes 400
  1610.0 34.6 %reduce-scatter.47.cloned.1.call-done = f32[192,768]{1,0:T(8,128)} async-done(((f32[768,768]{1,0:T(8,128)}), f32[192,768]{1,0:T(8,128)}) %reduce-scatter.47.cloned.1.call-update) | async-done | bytes 589840 | tf_op jit(solution)/shard_map/reduce_scatter | solution.py:264
  1644.6 35.8 %reduce-scatter.45.cloned.1.call-done = f32[192,768]{1,0:T(8,128)} async-done(((f32[768,768]{1,0:T(8,128)}), f32[192,768]{1,0:T(8,128)}) %reduce-scatter.45.cloned.1.call-update) | async-done | bytes 589840 | tf_op jit(solution)/shard_map/reduce_scatter | solution.py:257
  1680.4 25.2 %reduce-scatter.43.cloned.1.call-done = f32[48,768]{1,0:T(8,128)} async-done(((f32[192,768]{1,0:T(8,128)}), f32[48,768]{1,0:T(8,128)}) %reduce-scatter.43.cloned.1.call-update) | async-done | bytes 147472 | tf_op jit(solution)/shard_map/reduce_scatter | solution.py:253
  1705.6 32.8 %reduce-scatter.41.cloned.1.call-done = f32[192,576]{1,0:T(8,128)} async-done(((f32[768,576]{1,0:T(8,128)}), f32[192,576]{1,0:T(8,128)}) %reduce-scatter.41.cloned.1.call-update) | async-done | bytes 442384 | tf_op jit(solution)/shard_map/reduce_scatter | solution.py:251
  1738.4 20.2 %all-reduce = (f32[3642]{0:T(1024)S(1)}, f32[3642]{0:T(1024)S(1)}) all-reduce(f32[3642]{0:T(1024)S(1)} %get-tuple-element.185, f32[3642]{0:T(1024)S(1)} %get-tuple-element.186), channel_id=1, replica_groups=mesh['dp'=2,'row'=4,'col'=4] {'col'}, use_global_device_ids=true, to_apply=%region_26.27 | all-reduce | flops 7284 | bytes 58272 | tf_op jit(solution)/shard_map/psum | solution.py:74
  1758.7 83.7 %reduce-scatter.35.cloned.1.call-done = bf16[3642,192]{0,1:T(8,128)(2,1)} async-done(((bf16[3642,768]{0,1:T(8,128)(2,1)}), bf16[3642,192]{0,1:T(8,128)(2,1)}) %reduce-scatter.35.cloned.1.call-update) | async-done | bytes 1398544 | tf_op jit(solution)/shard_map/reduce_scatter | solution.py:193
  1842.4 6.6 multiply_add_fusion
  1849.0 5.0 copy.167
  1864.1 8.7 reshape.228
  1872.8 5.4 copy.168
  1887.1 8.7 all-reduce.2
  (359 shorter events, 281.6 us)
Async XLA Ops:
  8.0 180.9 %all-gather.15.cloned.1.call-start = ((), (), s32[]{:S(2)}) async-start(), calls=%async_computation.16 | async-start | bytes 7127040 | tf_op jit(solution)/shard_map/all_gather | solution.py:62
  21.2 61.8 %copy-start.25 = (f32[192]{0:T(256)}, f32[192]{0:T(256)S(1)}, u32[]{:S(2)}) copy-start(f32[192]{0:T(256)S(1)} %reshape.238) | copy-start | bytes 2308
  45.1 37.8 %copy-start.14 = (f32[3642]{0:T(1024)}, f32[3642]{0:T(1024)S(1)}, u32[]{:S(2)}) copy-start(f32[3642]{0:T(1024)S(1)} %broadcast_multiply_fusion.5) | copy-start | bytes 43708
  63.2 19.8 %copy-start.16 = (f32[3642]{0:T(1024)}, f32[3642]{0:T(1024)S(1)}, u32[]{:S(2)}) copy-start(f32[3642]{0:T(1024)S(1)} %add_rsqrt_fusion.1) | copy-start | bytes 43708
  83.0 23.5 %copy-start.2 = (f32[3642,192]{0,1:T(8,128)}, f32[3642,192]{0,1:T(8,128)S(1)}, u32[]{:S(2)}) copy-start(f32[3642,192]{0,1:T(8,128)S(1)} %copy.149) | copy-start | bytes 8391172
  83.0 1.7 copy-start.27
  83.0 7.2 copy-start.18
  83.0 7.2 copy-start.11
  84.6 418.0 %reduce-scatter.33.cloned.1.call-start = ((), (), s32[]{:S(2)}) async-start(), calls=%async_computation.17 | async-start | bytes 14254080 | tf_op jit(solution)/shard_map/reduce_scatter | solution.py:180
  294.1 17.2 copy-start.3
  311.3 1.1 copy-start.8
  311.3 1.9 copy-start.28
  311.3 1.9 copy-start.29
  311.3 1.9 copy-start.30
  311.4 258.2 %all-gather.19.cloned.1.call-start = ((), (), s32[]{:S(2)}) async-start(), calls=%async_computation.19 | async-start | bytes 1474560 | tf_op jit(solution)/shard_map/all_gather | solution.py:142
  313.2 332.9 %all-gather.17.cloned.1.call-start = ((), (), s32[]{:S(2)}) async-start(), calls=%async_computation.18 | async-start | bytes 7127040 | tf_op jit(solution)/shard_map/all_gather | solution.py:62
  323.8 706.2 %copy-start.23 = (f32[192]{0:T(256)}, f32[192]{0:T(256)S(1)}, u32[]{:S(2)}) copy-start(f32[192]{0:T(256)S(1)} %reshape.243) | copy-start | bytes 2308
  505.7 524.3 %copy-start = (f32[3642,192]{0,1:T(8,128)}, f32[3642,192]{0,1:T(8,128)S(1)}, u32[]{:S(2)}) copy-start(f32[3642,192]{0,1:T(8,128)S(1)} %get-tuple-element.238) | copy-start | bytes 8391172
  524.2 505.7 %copy-start.9 = (f32[3642]{0:T(1024)}, f32[3642]{0:T(1024)S(1)}, u32[]{:S(2)}) copy-start(f32[3642]{0:T(1024)S(1)} %broadcast_multiply_fusion.4) | copy-start | bytes 43708
  540.1 489.9 %copy-start.12 = (f32[3642]{0:T(1024)}, f32[3642]{0:T(1024)S(1)}, u32[]{:S(2)}) copy-start(f32[3642]{0:T(1024)S(1)} %add_rsqrt_fusion) | copy-start | bytes 43708
  541.8 121.9 %all-gather.21.cloned.1.call-start = ((), (), s32[]{:S(2)}) async-start(), calls=%async_computation.20 | async-start | bytes 1474560 | tf_op jit(solution)/shard_map/all_gather | solution.py:144
  543.7 227.1 %all-gather.23.cloned.1.call-start = ((), (), s32[]{:S(2)}) async-start(), calls=%async_computation.22 | async-start | bytes 7127040 | tf_op jit(solution)/shard_map/all_gather | solution.py:66
  560.5 3.9 copy-start.31
  564.3 443.1 %reduce-scatter.37.cloned.1.call-start = ((), (), s32[]{:S(2)}) async-start(), calls=%async_computation.23 | async-start | bytes 14254080 | tf_op jit(solution)/shard_map/reduce_scatter | solution.py:70
  770.8 38.0 %copy-start.34 = (bf16[768,768]{1,0:T(8,128)(2,1)S(1)}, bf16[768,768]{1,0:T(8,128)(2,1)}, u32[]{:S(2)}) copy-start(bf16[768,768]{1,0:T(8,128)(2,1)} %all-gather.19.cloned.1.call-done) | copy-start | bytes 3538948
  806.3 2.4 copy-start.35
  816.3 322.6 %all-gather.25.cloned.1.call-start = ((), (), s32[]{:S(2)}) async-start(), calls=%async_computation.24 | async-start | bytes 7127040 | tf_op jit(solution)/shard_map/all_gather | solution.py:66
  1029.9 4.8 copy-start.19
  1029.9 4.8 copy-start.21
  1034.7 439.6 %reduce-scatter.39.cloned.1.call-start = ((), (), s32[]{:S(2)}) async-start(), calls=%async_computation.25 | async-start | bytes 14254080 | tf_op jit(solution)/shard_map/reduce_scatter | solution.py:70
  1261.0 12.2 copy-start.7
  1283.0 1.4 copy-start.4
  1283.0 214.8 %reduce-scatter.55.cloned.1.call-start = ((), (), s32[]{:S(2)}) async-start(), calls=%async_computation.33 | async-start | bytes 40960
  1285.4 234.9 %reduce-scatter.53.cloned.1.call-start = ((), (), s32[]{:S(2)}) async-start(), calls=%async_computation.32 | async-start | bytes 163840
  1286.3 256.0 %reduce-scatter.63.cloned.1.call-start = ((), (), s32[]{:S(2)}) async-start(), calls=%async_computation.37 | async-start | bytes 40960
  1287.2 277.1 %reduce-scatter.61.cloned.1.call-start = ((), (), s32[]{:S(2)}) async-start(), calls=%async_computation.36 | async-start | bytes 40960
  1288.0 298.7 %reduce-scatter.51.cloned.1.call-start = ((), (), s32[]{:S(2)}) async-start(), calls=%async_computation.31 | async-start | bytes 40960
  1300.0 309.2 %reduce-scatter.49.cloned.1.call-start = ((), (), s32[]{:S(2)}) async-start(), calls=%async_computation.30 | async-start | bytes 81920
  1309.1 335.5 %reduce-scatter.47.cloned.1.call-start = ((), (), s32[]{:S(2)}) async-start(), calls=%async_computation.29 | async-start | bytes 2949120 | tf_op jit(solution)/shard_map/reduce_scatter | solution.py:264
  1320.0 10.6 copy-start.5
  1320.0 360.4 %reduce-scatter.45.cloned.1.call-start = ((), (), s32[]{:S(2)}) async-start(), calls=%async_computation.28 | async-start | bytes 2949120 | tf_op jit(solution)/shard_map/reduce_scatter | solution.py:257
  1330.6 375.0 %reduce-scatter.43.cloned.1.call-start = ((), (), s32[]{:S(2)}) async-start(), calls=%async_computation.27 | async-start | bytes 737280 | tf_op jit(solution)/shard_map/reduce_scatter | solution.py:253
  1335.9 10.3 copy-start.33
  1335.9 402.5 %reduce-scatter.41.cloned.1.call-start = ((), (), s32[]{:S(2)}) async-start(), calls=%async_computation.26 | async-start | bytes 2457600 | tf_op jit(solution)/shard_map/reduce_scatter | solution.py:251
  1346.2 496.2 %reduce-scatter.35.cloned.1.call-start = ((), (), s32[]{:S(2)}) async-start(), calls=%async_computation.21 | async-start | bytes 7127040 | tf_op jit(solution)/shard_map/reduce_scatter | solution.py:193
  1355.4 118.9 %copy-start.15 = (f32[3642]{0:T(1024)S(1)}, f32[3642]{0:T(1024)}, u32[]{:S(2)}) copy-start(f32[3642]{0:T(1024)} %copy-done.14) | copy-start | bytes 43708
  1355.4 118.9 %copy-start.17 = (f32[3642]{0:T(1024)S(1)}, f32[3642]{0:T(1024)}, u32[]{:S(2)}) copy-start(f32[3642]{0:T(1024)} %copy-done.16) | copy-start | bytes 43708
  1355.4 118.9 %copy-start.26 = (f32[192]{0:T(256)S(1)}, f32[192]{0:T(256)}, u32[]{:S(2)}) copy-start(f32[192]{0:T(256)} %copy-done.25) | copy-start | bytes 2308
  1355.4 124.2 %copy-start.32 = (f32[3,16]{1,0:T(4,128)S(1)}, f32[3,16]{1,0:T(4,128)}, u32[]{:S(2)}) copy-start(f32[3,16]{1,0:T(4,128)} %param.26) | copy-start | bytes 580
  1355.4 486.9 %copy-start.1 = (f32[3642,192]{0,1:T(8,128)S(1)}, f32[3642,192]{0,1:T(8,128)}, u32[]{:S(2)}) copy-start(f32[3642,192]{0,1:T(8,128)} %copy-done) | copy-start | bytes 8391172
  1355.4 486.9 %copy-start.10 = (f32[3642]{0:T(1024)S(1)}, f32[3642]{0:T(1024)}, u32[]{:S(2)}) copy-start(f32[3642]{0:T(1024)} %copy-done.9) | copy-start | bytes 43708
  1355.5 486.9 %copy-start.13 = (f32[3642]{0:T(1024)S(1)}, f32[3642]{0:T(1024)}, u32[]{:S(2)}) copy-start(f32[3642]{0:T(1024)} %copy-done.12) | copy-start | bytes 43708
  1355.5 486.9 %copy-start.20 = (f32[3642]{0:T(1024)S(1)}, f32[3642]{0:T(1024)}, u32[]{:S(2)}) copy-start(f32[3642]{0:T(1024)} %copy-done.19) | copy-start | bytes 43708
  1355.5 486.9 %copy-start.22 = (f32[3642]{0:T(1024)S(1)}, f32[3642]{0:T(1024)}, u32[]{:S(2)}) copy-start(f32[3642]{0:T(1024)} %copy-done.21) | copy-start | bytes 43708
  1355.5 486.9 %copy-start.24 = (f32[192]{0:T(256)S(1)}, f32[192]{0:T(256)}, u32[]{:S(2)}) copy-start(f32[192]{0:T(256)} %copy-done.23) | copy-start | bytes 2308
  1355.5 525.1 %reduce-scatter.59.cloned.1.call-start = ((), (), s32[]{:S(2)}) async-start(), calls=%async_computation.35 | async-start | bytes 40960
  1479.6 406.7 %reduce-scatter.57.cloned.1.call-start = ((), (), s32[]{:S(2)}) async-start(), calls=%async_computation.34 | async-start | bytes 40960
  1485.6 410.2 %all-reduce.6.cloned.1.call-start = ((), (), s32[]{:S(2)}) async-start(), calls=%async_computation.38 | async-start | bytes 3637248 | tf_op jit(solution)/shard_map/psum | solution.py:281
  1849.0 5.0 copy-start.6
Sparse Core Ops, SparseCore 0:
  84.8 104.1 all-gather.14
  311.5 191.0 reduce-scatter.32
  1034.8 104.0 all-gather.24
  1283.1 191.1 reduce-scatter.38
  1477.1 20.6 reduce-scatter.54
  1500.6 19.6 reduce-scatter.52
  1522.7 19.5 reduce-scatter.62
  1544.7 19.5 reduce-scatter.60
  1567.2 19.5 reduce-scatter.50
  1589.6 19.5 reduce-scatter.48
  1611.7 32.8 reduce-scatter.46
  1647.5 32.8 reduce-scatter.44
  1683.5 22.0 reduce-scatter.42
  1708.0 30.3 reduce-scatter.40
  1740.6 101.7 reduce-scatter.34
  1844.6 19.8 reduce-scatter.58
  1866.7 19.5 reduce-scatter.56
Sparse Core Ops, SparseCore 1:
  314.0 15.6 all-gather.18
  541.9 104.1 all-gather.16
  648.1 15.5 all-gather.20
  665.3 105.4 all-gather.22
  816.4 191.0 reduce-scatter.36
  1738.5 56.7 all-reduce.5
where the time goes:
time: 1920 us; the launch traced here: 1910 us
  waiting for transfers between devices  1200 us (62%)
  matrix products  251 us (13%)
  local copies, waits for them, and re-layouts  193 us (10%)
  blocking collectives  175 us (9%)
  other arithmetic  76.7 us (4%)
    reduce_scatter x2, waiting for transfers between devices, norm_back(): lax.psum_scatter(partial_rows, 'col', scatter_dimension=1, tiled=True)  310 us
    all_gather x2, waiting for transfers between devices, gather_grads(): return lax.all_gather(values, 'col', axis=1, tiled=True)  211 us
    reduce_scatter x1, waiting for transfers between devices, body(): lax.psum_scatter(jnp.dot(heads, merge_mat, preferred_element_type=jnp.flo...  174 us
    all_gather x2, waiting for transfers between devices, spread_rows(): return lax.all_gather(values, 'col', axis=1, tiled=True)  159 us
    unnamed x31, waiting for transfers between devices  125 us
    dot_general x31, matrix products, times_transposed(): lax.dot_general(left, right, (((1,), (1,)), ((), ())), preferred_element_...  111 us
    reduce_scatter x1, waiting for transfers between devices, body(): lax.psum_scatter(jnp.dot(active, reduce_mat, preferred_element_type=jnp.f...  83.7 us
    psum x4, blocking collectives, row_sum(): return lax.psum(values, 'col')  68.8 us
  transfers between devices with their start and end apart: 23, of which 20 were waited for; matrix products, arithmetic and copies ran while one was open for 8% of the time, Pallas kernels for 0%

commit v1 on v0

--- a/solution.py
+++ b/solution.py
@@ -1,3 +1,4 @@
+import functools
 import jax
 import jax.numpy as jnp
 from jax import lax
@@ -7,6 +8,25 @@
 HD = 64
 LEN = 1214
 EPSILON = 1e-06
+
+
+def end_the_positions(x_in, row_axis):
+    axis_len = lax.axis_size(row_axis)
+    pool = [(p, (p + 1) % axis_len) for p in range(axis_len)]
+    line_up = [(p, (p - 1) % axis_len) for p in range(axis_len)]
+    piece_now, answer = ([x_in], [x_in])
+    for _ in range(axis_len // 2):
+        n_now = lax.ppermute(piece_now[-1], row_axis, perm=pool)
+        piece_now.append(n_now)
+    for _ in range((axis_len - 1) // 2):
+        val = lax.ppermute(answer[-1], perm=line_up, axis_name=row_axis)
+        answer.append(val)
+    v1 = jnp.concatenate([*piece_now[::-1], *answer[1:]], axis=1)
+    all_values = lax.axis_index(row_axis)
+    return jnp.roll(v1, shift=(all_values - axis_len // 2) * x_in.shape[1], axis=1)
+
+
+_tell_column = functools.partial(end_the_positions, row_axis="col")
 
 
 def to_rows(values):
@@ -63,7 +83,7 @@
 
 
 def gather_grads(values):
-    return lax.all_gather(values, "col", axis=1, tiled=True)
+    return _tell_column(values)
 
 
 def norm_back(partial_rows, scaled, inverse, gain):

time: 1920 us -> 1950 us (1.016)
  waiting for transfers between devices: 1200 us -> 1070 us
  starting transfers between devices: 1.72 us -> 84 us
  other arithmetic: 76.7 us -> 137 us
    all_gather x2 -> x0, waiting for transfers between devices: 211 us -> none  [gather_grads(): return lax.all_gather(values, 'col', axis=1, tiled=True)]
    ppermute x0 -> x6, waiting for transfers between devices: none -> 171 us  [the longest x4 167 us: end_the_positions(): n_now = lax.ppermute(piece_now[-1], row_axis, perm=pool)]
    ppermute x0 -> x6, starting transfers between devices: none -> 82.4 us  [the longest x4 74.8 us: end_the_positions(): n_now = lax.ppermute(piece_now[-1], row_axis, perm=pool)]
    all_gather x2, waiting for transfers between devices: 159 us -> 82.4 us  [spread_rows(): return lax.all_gather(values, 'col', axis=1, tiled=True)]
    concatenate x0 -> x2, other arithmetic: none -> 60 us  [end_the_positions(): jnp.roll(v1, shift=(all_values - axis_len // 2) * x_in.shape[1], axis=1)]
    unnamed x31 -> x29, waiting for transfers between devices: 125 us -> 125 us
  transfers between devices with their start and end apart: 23 -> 27, of which waited for: 20 -> 21; matrix products, arithmetic and copies ran while one was open for 8% -> 10% of each run, Pallas kernels for 0% -> 0%
where the time goes in v1:
time: 1950 us; the launch traced here: 1940 us
  waiting for transfers between devices  1070 us (55%)
  matrix products  246 us (13%)
  local copies, waits for them, and re-layouts  206 us (11%)
  blocking collectives  174 us (9%)
  other arithmetic  137 us (7%)
  starting transfers between devices  84 us (4%)
    reduce_scatter x2, waiting for transfers between devices, norm_back(): lax.psum_scatter(partial_rows, 'col', scatter_dimension=1, tiled=True)  311 us
    reduce_scatter x1, waiting for transfers between devices, body(): lax.psum_scatter(jnp.dot(heads, merge_mat, preferred_element_type=jnp.flo...  174 us
    ppermute x4, waiting for transfers between devices, end_the_positions(): n_now = lax.ppermute(piece_now[-1], row_axis, perm=pool)  167 us
    unnamed x29, waiting for transfers between devices  125 us
    dot_general x31, matrix products, times_transposed(): lax.dot_general(left, right, (((1,), (1,)), ((), ())), preferred_element_...  105 us
    reduce_scatter x1, waiting for transfers between devices, body(): lax.psum_scatter(jnp.dot(active, reduce_mat, preferred_element_type=jnp.f...  83.9 us
    all_gather x2, waiting for transfers between devices, spread_rows(): return lax.all_gather(values, 'col', axis=1, tiled=True)  82.4 us
    ppermute x4, starting transfers between devices, end_the_positions(): n_now = lax.ppermute(piece_now[-1], row_axis, perm=pool)  74.8 us
  transfers between devices with their start and end apart: 27, of which 21 were waited for; matrix products, arithmetic and copies ran while one was open for 10% of the time, Pallas kernels for 0%

profile of v1, /device:TPU:0, one launch (start us, length us, event | category | flops | bytes accessed | tf_op | source)
XLA Modules:
  0.0 1939.3 jit_solution(14020042399139519086)
XLA Ops:
  9.4 6.0 all-gather.1
  15.6 5.4 all-gather
  26.0 19.2 psum.140
  47.6 15.6 psum.141
  63.2 7.0 copy.138
  70.2 9.2 reshape.237
  85.1 5.1 all-gather.2
  90.7 6.0 all_gather.47
  96.7 10.2 all_gather.45
  106.9 82.4 %all-gather.13.cloned.1.call-done = bf16[3642,768]{0,1:T(8,128)(2,1)} async-done(((bf16[3642,192]{0,1:T(8,128)(2,1)}), bf16[3642,768]{0,1:T(8,128)(2,1)}) %all-gather.13.cloned.1.call-update) | async-done | bytes 5594128 | tf_op jit(solution)/shard_map/all_gather | solution.py:82
  189.3 8.5 add_convert_fusion.1
  197.9 14.5 reshape.217
  212.4 5.4 fusion.73
  225.4 5.2 copy.179
  230.6 64.2 %while.22 = (s32[]{:T(128)}, bf16[9,1214,64]{1,2,0:T(8,128)(2,1)}, f32[9,1214]{1,0:T(8,128)}, bf16[9,1214,64]{2,1,0:T(8,128)(2,1)}, bf16[9,1214,64]{2,1,0:T(8,12...) while((s32[]{:T(128)}, bf16[9,1214,64]{1,2,0:T(8,128)(2,1)}, f32[9,1214]{1,0:T(8,128)}, ...), condition=%wide.region_7.8_spmd, body=%wide.region_4.7_spmd.sunk | while | flops 387684832 | bytes 18843696 | solution.py:194
  304.6 7.4 fusion.76
  324.5 5.1 all-gather.3
  329.8 173.6 %reduce-scatter.33.cloned.1.call-done = f32[3642,192]{0,1:T(8,128)} async-done(((f32[3642,768]{0,1:T(8,128)}), f32[3642,192]{0,1:T(8,128)}) %reduce-scatter.33.cloned.1.call-update) | async-done | bytes 2797072 | tf_op jit(solution)/shard_map/reduce_scatter | solution.py:200
  506.4 18.5 psum.142
  525.3 15.5 psum.143
  545.3 6.0 copy.162
  551.3 7.9 reshape.223
  566.8 62.9 %collective-permute-done = bf16[3642,192]{0,1:T(8,128)(2,1)} collective-permute-done((bf16[3642,192]{0,1:T(8,128)(2,1)}, bf16[3642,192]{0,1:T(8,128)(2,1)}, u32[]{:S(2)}, u32[]{:S(2)}) %collective-permute-start) | collective-permute-done | bytes 1398560 | tf_op jit(solution)/shard_map/ppermute | solution.py:19
  629.7 51.7 %collective-permute-start.1 = (bf16[3642,192]{0,1:T(8,128)(2,1)}, bf16[3642,192]{0,1:T(8,128)(2,1)}, u32[]{:S(2)}, u32[]{:S(2)}) collective-permute-start(bf16[3642,192]{0,1:T(8,128)(2,1)} %collective-permute-done), channel_id=1, source_target_pairs={{0,1},{1,2},{2,3},{3,0},{4,5},{5,6},{6,7},{7,4},{8,9},{9,10},{10,1... | collective-permute-start | bytes 4195592 | tf_op jit(solution)/shard_map/ppermute | solution.py:19
  695.8 42.1 %collective-permute-done.1 = bf16[3642,192]{0,1:T(8,128)(2,1)} collective-permute-done((bf16[3642,192]{0,1:T(8,128)(2,1)}, bf16[3642,192]{0,1:T(8,128)(2,1)}, u32[]{:S(2)}, u32[]{:S(2)}) %collective-permute-start.1) | collective-permute-done | bytes 1398560 | tf_op jit(solution)/shard_map/ppermute | solution.py:19
  741.5 31.6 %fusion.63 = bf16[3642,768]{1,0:T(8,128)(2,1)} fusion(s32[]{:T(128)S(6)} %select_n.13, bf16[3642,192]{1,0:T(8,128)(2,1)} %copy.166, bf16[3642,192]{1,0:T(8,128)(2,1)} %copy.167, bf16[3642,192]{1,0:T(8,128)(2,1)} %reshape.223, bf16[3642,192]{1,0:T(8,128)(2,1)} %copy.168), kind=kLoop, calls=%fused_computation.102 | loop fusion | flops 44752896 | bytes 11188228 | tf_op jit(solution)/shard_map/jit(_roll_dynamic)/concatenate | solution.py:26
  773.1 11.6 fusion.77
  784.8 32.6 %convert_reduce_fusion.1 = (f32[768]{0:T(1024)S(1)}, bf16[3642,768]{1,0:T(8,128)(2,1)S(1)}, f32[3642,768]{1,0:T(8,128)}) fusion(f32[3642,768]{1,0:T(8,128)} %fusion.77, f32[768]{0:T(1024)S(1)} %reshape.245, bf16[3642,768]{1,0:T(8,128)(2,1)} %fusion.63, bf16[768,768]{1,0:T(8,128)(2,1)} %all-gather.19.cloned.1.call-done), kind=kOutput, calls=%fused_computation.73 | convolution fusion | flops 4506056704 | bytes 34750464 | tf_op jit(solution)/shard_map/dot_general | solution.py:59
  819.8 7.5 fusion.78
  827.4 192.1 %reduce-scatter.37.cloned.1.call-done = f32[3642,192]{0,1:T(8,128)} async-done(((f32[3642,768]{0,1:T(8,128)}), f32[3642,192]{0,1:T(8,128)}) %reduce-scatter.37.cloned.1.call-update) | async-done | bytes 2797072 | tf_op jit(solution)/shard_map/reduce_scatter | solution.py:90
  1023.1 18.8 all-reduce.1
  1050.5 32.3 %collective-permute-done.3 = bf16[3642,192]{0,1:T(8,128)(2,1)S(1)} collective-permute-done((bf16[3642,192]{0,1:T(8,128)(2,1)}, bf16[3642,192]{0,1:T(8,128)(2,1)S(1)}, u32[]{:S(2)}, u32[]{:S(2)}) %collective-permute-start.3) | collective-permute-done | bytes 1398560 | tf_op jit(solution)/shard_map/ppermute | solution.py:19
  1082.8 23.1 %collective-permute-start.4 = (bf16[3642,192]{0,1:T(8,128)(2,1)S(1)}, bf16[3642,192]{0,1:T(8,128)(2,1)}, u32[]{:S(2)}, u32[]{:S(2)}) collective-permute-start(bf16[3642,192]{0,1:T(8,128)(2,1)S(1)} %collective-permute-done.3), channel_id=1, source_target_pairs={{0,1},{1,2},{2,3},{3,0},{4,5},{5,6},{6,7},{7,4},{8,9},{9,10},{10,1... | collective-permute-start | bytes 4195592 | tf_op jit(solution)/shard_map/ppermute | solution.py:19
  1109.7 29.6 %collective-permute-done.4 = bf16[3642,192]{0,1:T(8,128)(2,1)} collective-permute-done((bf16[3642,192]{0,1:T(8,128)(2,1)S(1)}, bf16[3642,192]{0,1:T(8,128)(2,1)}, u32[]{:S(2)}, u32[]{:S(2)}) %collective-permute-start.4) | collective-permute-done | bytes 1398560 | tf_op jit(solution)/shard_map/ppermute | solution.py:19
  1139.3 28.5 %fusion.56 = bf16[3642,768]{0,1:T(8,128)(2,1)S(1)} fusion(s32[]{:T(128)S(6)} %select_n.13, bf16[3642,192]{0,1:T(8,128)(2,1)} %collective-permute-done.4, bf16[3642,192]{0,1:T(8,128)(2,1)S(1)} %collective-permute-done.3, bf16[3642,192]{0,1:T(8,128)(2,1)} %get-tuple-element.237, bf16[3642,192]{0,1:T(8,128)(2,1)S(1)} %collective-permute-done.5), kind=kLoop, calls=%fused_computation.95 | loop fusion | flops 44752896 | bytes 11188228 | tf_op jit(solution)/shard_map/jit(_roll_dynamic)/concatenate | solution.py:26
  1179.0 102.5 %while.23 = (s32[]{:T(128)}, bf16[9,1214,3,64]{1,3,2,0:T(8,128)(2,1)}, bf16[9,1214,64]{2,1,0:T(8,128)(2,1)}, bf16[9,1214,64]{2,1,0:T(8,128)(2,1)}, f32[9,1214]{1...) while((s32[]{:T(128)}, ...), condition=%wide.region_21.23_spmd, body=%wide.region_19.22_spmd.sunk | while | flops 956805568 | bytes 48504736 | solution.py:242
  1281.5 8.6 copy.215
  1290.0 12.2 reshape.227
  1302.3 9.6 fusion.79
  1317.4 10.9 multiply_convert_fusion.1
  1329.2 8.2 convert_reduce_fusion
  1338.2 10.5 fusion.83
  1349.0 10.5 fusion.82
  1359.6 5.2 fusion.81
  1364.9 10.0 fusion.80
  1374.9 9.2 convolution_convert_fusion
  1384.5 118.5 %reduce-scatter.39.cloned.1.call-done = f32[3642,192]{0,1:T(8,128)} async-done(((f32[3642,768]{0,1:T(8,128)}), f32[3642,192]{0,1:T(8,128)}) %reduce-scatter.39.cloned.1.call-update) | async-done | bytes 2797072 | tf_op jit(solution)/shard_map/reduce_scatter | solution.py:90
  1514.4 11.9 reduce-scatter.55.cloned.1.call-done
  1527.2 21.8 %reduce-scatter.53.cloned.1.call-done = f32[64,3]{1,0:T(8,128)} async-done(((f32[256,3]{1,0:T(8,128)}), f32[64,3]{1,0:T(8,128)}) %reduce-scatter.53.cloned.1.call-update) | async-done | bytes 784
  1549.7 21.0 %reduce-scatter.63.cloned.1.call-done = f32[16,3]{1,0:T(8,128)} async-done(((f32[64,3]{1,0:T(8,128)}), f32[16,3]{1,0:T(8,128)}) %reduce-scatter.63.cloned.1.call-update) | async-done | bytes 208
  1571.5 21.2 %reduce-scatter.61.cloned.1.call-done = f32[16,3]{1,0:T(8,128)} async-done(((f32[64,3]{1,0:T(8,128)}), f32[16,3]{1,0:T(8,128)}) %reduce-scatter.61.cloned.1.call-update) | async-done | bytes 208
  1593.5 21.8 %reduce-scatter.51.cloned.1.call-done = f32[16,3]{1,0:T(8,128)} async-done(((f32[64,3]{1,0:T(8,128)}), f32[16,3]{1,0:T(8,128)}) %reduce-scatter.51.cloned.1.call-update) | async-done | bytes 208
  1616.0 21.8 %reduce-scatter.49.cloned.1.call-done = f32[32,3]{1,0:T(8,128)} async-done(((f32[128,3]{1,0:T(8,128)}), f32[32,3]{1,0:T(8,128)}) %reduce-scatter.49.cloned.1.call-update) | async-done | bytes 400
  1638.6 34.4 %reduce-scatter.47.cloned.1.call-done = f32[192,768]{1,0:T(8,128)} async-done(((f32[768,768]{1,0:T(8,128)}), f32[192,768]{1,0:T(8,128)}) %reduce-scatter.47.cloned.1.call-update) | async-done | bytes 589840 | tf_op jit(solution)/shard_map/reduce_scatter | solution.py:284
  1673.0 36.0 %reduce-scatter.45.cloned.1.call-done = f32[192,768]{1,0:T(8,128)} async-done(((f32[768,768]{1,0:T(8,128)}), f32[192,768]{1,0:T(8,128)}) %reduce-scatter.45.cloned.1.call-update) | async-done | bytes 589840 | tf_op jit(solution)/shard_map/reduce_scatter | solution.py:277
  1709.0 25.0 %reduce-scatter.43.cloned.1.call-done = f32[48,768]{1,0:T(8,128)} async-done(((f32[192,768]{1,0:T(8,128)}), f32[48,768]{1,0:T(8,128)}) %reduce-scatter.43.cloned.1.call-update) | async-done | bytes 147472 | tf_op jit(solution)/shard_map/reduce_scatter | solution.py:273
  1734.0 33.0 %reduce-scatter.41.cloned.1.call-done = f32[192,576]{1,0:T(8,128)} async-done(((f32[768,576]{1,0:T(8,128)}), f32[192,576]{1,0:T(8,128)}) %reduce-scatter.41.cloned.1.call-update) | async-done | bytes 442384 | tf_op jit(solution)/shard_map/reduce_scatter | solution.py:271
  1767.0 20.0 %all-reduce = (f32[3642]{0:T(1024)S(1)}, f32[3642]{0:T(1024)S(1)}) all-reduce(f32[3642]{0:T(1024)S(1)} %get-tuple-element.186, f32[3642]{0:T(1024)S(1)} %get-tuple-element.187), channel_id=1, replica_groups=mesh['dp'=2,'row'=4,'col'=4] {'col'}, use_global_device_ids=true, to_apply=%region_26.28 | all-reduce | flops 7284 | bytes 58272 | tf_op jit(solution)/shard_map/psum | solution.py:94
  1787.0 83.9 %reduce-scatter.35.cloned.1.call-done = bf16[3642,192]{0,1:T(8,128)(2,1)} async-done(((bf16[3642,768]{0,1:T(8,128)(2,1)}), bf16[3642,192]{0,1:T(8,128)(2,1)}) %reduce-scatter.35.cloned.1.call-update) | async-done | bytes 1398544 | tf_op jit(solution)/shard_map/reduce_scatter | solution.py:213
  1871.0 6.6 multiply_add_fusion
  1892.7 8.7 reshape.228
  1901.4 5.4 copy.176
  1909.9 5.1 reduce-scatter.57.cloned.1.call-done
  1915.8 8.7 all-reduce.2
  (372 shorter events, 324.3 us)
Async XLA Ops:
  8.0 181.3 %all-gather.13.cloned.1.call-start = ((), (), s32[]{:S(2)}) async-start(), calls=%async_computation.16 | async-start | bytes 7127040 | tf_op jit(solution)/shard_map/all_gather | solution.py:82
  21.2 61.8 %copy-start.26 = (f32[192]{0:T(256)}, f32[192]{0:T(256)S(1)}, u32[]{:S(2)}) copy-start(f32[192]{0:T(256)S(1)} %reshape.238) | copy-start | bytes 2308
  45.1 37.9 %copy-start.15 = (f32[3642]{0:T(1024)}, f32[3642]{0:T(1024)S(1)}, u32[]{:S(2)}) copy-start(f32[3642]{0:T(1024)S(1)} %broadcast_multiply_fusion.5) | copy-start | bytes 43708
  63.2 19.9 %copy-start.17 = (f32[3642]{0:T(1024)}, f32[3642]{0:T(1024)S(1)}, u32[]{:S(2)}) copy-start(f32[3642]{0:T(1024)S(1)} %add_rsqrt_fusion.1) | copy-start | bytes 43708
  79.4 5.7 copy-start.28
  79.4 11.2 copy-start.19
  79.4 11.2 copy-start.12
  83.0 114.8 %copy-start.2 = (f32[3642,192]{0,1:T(8,128)}, f32[3642,192]{0,1:T(8,128)S(1)}, u32[]{:S(2)}) copy-start(f32[3642,192]{0,1:T(8,128)S(1)} %copy.153) | copy-start | bytes 8391172
  85.1 418.3 %reduce-scatter.33.cloned.1.call-start = ((), (), s32[]{:S(2)}) async-start(), calls=%async_computation.17 | async-start | bytes 14254080 | tf_op jit(solution)/shard_map/reduce_scatter | solution.py:200
  294.8 17.2 copy-start.3
  312.0 1.1 copy-start.9
  312.0 1.9 copy-start.29
  312.0 1.9 copy-start.30
  312.0 1.9 copy-start.31
  312.1 461.0 %all-gather.17.cloned.1.call-start = ((), (), s32[]{:S(2)}) async-start(), calls=%async_computation.19 | async-start | bytes 1474560 | tf_op jit(solution)/shard_map/all_gather | solution.py:162
  313.9 459.3 %all-gather.15.cloned.1.call-start = ((), (), s32[]{:S(2)}) async-start(), calls=%async_computation.18 | async-start | bytes 7127040 | tf_op jit(solution)/shard_map/all_gather | solution.py:82
  324.5 717.5 %copy-start.24 = (f32[192]{0:T(256)}, f32[192]{0:T(256)S(1)}, u32[]{:S(2)}) copy-start(f32[192]{0:T(256)S(1)} %reshape.243) | copy-start | bytes 2308
  506.4 535.6 %copy-start = (f32[3642,192]{0,1:T(8,128)}, f32[3642,192]{0,1:T(8,128)S(1)}, u32[]{:S(2)}) copy-start(f32[3642,192]{0,1:T(8,128)S(1)} %get-tuple-element.239) | copy-start | bytes 8391172
  524.9 517.0 %copy-start.10 = (f32[3642]{0:T(1024)}, f32[3642]{0:T(1024)S(1)}, u32[]{:S(2)}) copy-start(f32[3642]{0:T(1024)S(1)} %broadcast_multiply_fusion.4) | copy-start | bytes 43708
  540.8 501.2 %copy-start.13 = (f32[3642]{0:T(1024)}, f32[3642]{0:T(1024)S(1)}, u32[]{:S(2)}) copy-start(f32[3642]{0:T(1024)S(1)} %add_rsqrt_fusion) | copy-start | bytes 43708
  542.5 242.3 %all-gather.19.cloned.1.call-start = ((), (), s32[]{:S(2)}) async-start(), calls=%async_computation.20 | async-start | bytes 1474560 | tf_op jit(solution)/shard_map/all_gather | solution.py:164
  551.3 131.9 %copy-start.32 = (f32[3,64]{1,0:T(4,128)S(1)}, f32[3,64]{1,0:T(4,128)}, u32[]{:S(2)}) copy-start(f32[3,64]{1,0:T(4,128)} %param.26) | copy-start | bytes 2308
  562.9 66.8 %collective-permute-start = (bf16[3642,192]{0,1:T(8,128)(2,1)}, bf16[3642,192]{0,1:T(8,128)(2,1)}, u32[]{:S(2)}, u32[]{:S(2)}) collective-permute-start(bf16[3642,192]{0,1:T(8,128)(2,1)} %copy.163), channel_id=1, source_target_pairs={{0,1},{1,2},{2,3},{3,0},{4,5},{5,6},{6,7},{7,4},{8,9},{9,10},{10,1... | collective-permute-start | bytes 4195592 | tf_op jit(solution)/shard_map/ppermute | solution.py:19
  563.0 129.1 %collective-permute-start.2 = (bf16[3642,192]{0,1:T(8,128)(2,1)}, bf16[3642,192]{0,1:T(8,128)(2,1)}, u32[]{:S(2)}, u32[]{:S(2)}) collective-permute-start(bf16[3642,192]{0,1:T(8,128)(2,1)} %copy.163), channel_id=1, source_target_pairs={{0,3},{1,0},{2,1},{3,2},{4,7},{5,4},{6,5},{7,6},{8,11},{9,8},{10,9... | collective-permute-start | bytes 4195592 | tf_op jit(solution)/shard_map/ppermute | solution.py:22
  629.7 108.2 %collective-permute-start.1 = (bf16[3642,192]{0,1:T(8,128)(2,1)}, bf16[3642,192]{0,1:T(8,128)(2,1)}, u32[]{:S(2)}, u32[]{:S(2)}) collective-permute-start(bf16[3642,192]{0,1:T(8,128)(2,1)} %collective-permute-done), channel_id=1, source_target_pairs={{0,1},{1,2},{2,3},{3,0},{4,5},{5,6},{6,7},{7,4},{8,9},{9,10},{10,1... | collective-permute-start | bytes 4195592 | tf_op jit(solution)/shard_map/ppermute | solution.py:19
  683.2 336.3 %reduce-scatter.37.cloned.1.call-start = ((), (), s32[]{:S(2)}) async-start(), calls=%async_computation.22 | async-start | bytes 14254080 | tf_op jit(solution)/shard_map/reduce_scatter | solution.py:90
  784.8 35.0 %copy-start.35 = (bf16[768,768]{1,0:T(8,128)(2,1)S(1)}, bf16[768,768]{1,0:T(8,128)(2,1)}, u32[]{:S(2)}) copy-start(bf16[768,768]{1,0:T(8,128)(2,1)} %all-gather.17.cloned.1.call-done) | copy-start | bytes 3538948
  817.4 2.4 copy-start.36
  827.4 675.6 %reduce-scatter.39.cloned.1.call-start = ((), (), s32[]{:S(2)}) async-start(), calls=%async_computation.23 | async-start | bytes 14254080 | tf_op jit(solution)/shard_map/reduce_scatter | solution.py:90
  1041.9 40.9 %copy-start.20 = (f32[3642]{0:T(1024)}, f32[3642]{0:T(1024)S(1)}, u32[]{:S(2)}) copy-start(f32[3642]{0:T(1024)S(1)} %get-tuple-element.253) | copy-start | bytes 43708
  1041.9 40.9 %copy-start.22 = (f32[3642]{0:T(1024)}, f32[3642]{0:T(1024)S(1)}, u32[]{:S(2)}) copy-start(f32[3642]{0:T(1024)S(1)} %get-tuple-element.254) | copy-start | bytes 43708
  1046.7 36.1 %collective-permute-start.3 = (bf16[3642,192]{0,1:T(8,128)(2,1)}, bf16[3642,192]{0,1:T(8,128)(2,1)S(1)}, u32[]{:S(2)}, u32[]{:S(2)}) collective-permute-start(bf16[3642,192]{0,1:T(8,128)(2,1)} %get-tuple-element.237), channel_id=1, source_target_pairs={{0,1},{1,2},{2,3},{3,0},{4,5},{5,6},{6,7},{7,4},{8,9},{9,10},{10,1... | collective-permute-start | bytes 4195592 | tf_op jit(solution)/shard_map/ppermute | solution.py:19
  1046.7 63.0 %collective-permute-start.5 = (bf16[3642,192]{0,1:T(8,128)(2,1)}, bf16[3642,192]{0,1:T(8,128)(2,1)S(1)}, u32[]{:S(2)}, u32[]{:S(2)}) collective-permute-start(bf16[3642,192]{0,1:T(8,128)(2,1)} %get-tuple-element.237), channel_id=1, source_target_pairs={{0,3},{1,0},{2,1},{3,2},{4,7},{5,4},{6,5},{7,6},{8,11},{9,8},{10,9... | collective-permute-start | bytes 4195592 | tf_op jit(solution)/shard_map/ppermute | solution.py:22
  1082.8 56.5 %collective-permute-start.4 = (bf16[3642,192]{0,1:T(8,128)(2,1)S(1)}, bf16[3642,192]{0,1:T(8,128)(2,1)}, u32[]{:S(2)}, u32[]{:S(2)}) collective-permute-start(bf16[3642,192]{0,1:T(8,128)(2,1)S(1)} %collective-permute-done.3), channel_id=1, source_target_pairs={{0,1},{1,2},{2,3},{3,0},{4,5},{5,6},{6,7},{7,4},{8,9},{9,10},{10,1... | collective-permute-start | bytes 4195592 | tf_op jit(solution)/shard_map/ppermute | solution.py:19
  1167.8 2.4 copy-start.6
  1290.0 12.2 copy-start.8
  1311.9 1.4 copy-start.4
  1311.9 214.5 %reduce-scatter.55.cloned.1.call-start = ((), (), s32[]{:S(2)}) async-start(), calls=%async_computation.31 | async-start | bytes 40960
  1314.3 234.6 %reduce-scatter.53.cloned.1.call-start = ((), (), s32[]{:S(2)}) async-start(), calls=%async_computation.30 | async-start | bytes 163840
  1315.2 255.6 %reduce-scatter.63.cloned.1.call-start = ((), (), s32[]{:S(2)}) async-start(), calls=%async_computation.35 | async-start | bytes 40960
  1316.4 276.2 %reduce-scatter.61.cloned.1.call-start = ((), (), s32[]{:S(2)}) async-start(), calls=%async_computation.34 | async-start | bytes 40960
  1317.3 297.9 %reduce-scatter.51.cloned.1.call-start = ((), (), s32[]{:S(2)}) async-start(), calls=%async_computation.29 | async-start | bytes 40960
  1329.1 308.7 %reduce-scatter.49.cloned.1.call-start = ((), (), s32[]{:S(2)}) async-start(), calls=%async_computation.28 | async-start | bytes 81920
  1338.1 334.9 %reduce-scatter.47.cloned.1.call-start = ((), (), s32[]{:S(2)}) async-start(), calls=%async_computation.27 | async-start | bytes 2949120 | tf_op jit(solution)/shard_map/reduce_scatter | solution.py:284
  1348.7 10.8 copy-start.5
  1348.8 360.3 %reduce-scatter.45.cloned.1.call-start = ((), (), s32[]{:S(2)}) async-start(), calls=%async_computation.26 | async-start | bytes 2949120 | tf_op jit(solution)/shard_map/reduce_scatter | solution.py:277
  1359.5 374.5 %reduce-scatter.43.cloned.1.call-start = ((), (), s32[]{:S(2)}) async-start(), calls=%async_computation.25 | async-start | bytes 737280 | tf_op jit(solution)/shard_map/reduce_scatter | solution.py:273
  1364.8 10.1 copy-start.34
  1364.8 402.2 %reduce-scatter.41.cloned.1.call-start = ((), (), s32[]{:S(2)}) async-start(), calls=%async_computation.24 | async-start | bytes 2457600 | tf_op jit(solution)/shard_map/reduce_scatter | solution.py:271
  1374.9 496.1 %reduce-scatter.35.cloned.1.call-start = ((), (), s32[]{:S(2)}) async-start(), calls=%async_computation.21 | async-start | bytes 7127040 | tf_op jit(solution)/shard_map/reduce_scatter | solution.py:213
  1384.1 118.9 %copy-start.16 = (f32[3642]{0:T(1024)S(1)}, f32[3642]{0:T(1024)}, u32[]{:S(2)}) copy-start(f32[3642]{0:T(1024)} %copy-done.15) | copy-start | bytes 43708
  1384.1 118.9 %copy-start.18 = (f32[3642]{0:T(1024)S(1)}, f32[3642]{0:T(1024)}, u32[]{:S(2)}) copy-start(f32[3642]{0:T(1024)} %copy-done.17) | copy-start | bytes 43708
  1384.1 118.9 %copy-start.27 = (f32[192]{0:T(256)S(1)}, f32[192]{0:T(256)}, u32[]{:S(2)}) copy-start(f32[192]{0:T(256)} %copy-done.26) | copy-start | bytes 2308
  1384.1 124.2 %copy-start.33 = (f32[3,16]{1,0:T(4,128)S(1)}, f32[3,16]{1,0:T(4,128)}, u32[]{:S(2)}) copy-start(f32[3,16]{1,0:T(4,128)} %param.28) | copy-start | bytes 580
  1384.1 486.8 %copy-start.1 = (f32[3642,192]{0,1:T(8,128)S(1)}, f32[3642,192]{0,1:T(8,128)}, u32[]{:S(2)}) copy-start(f32[3642,192]{0,1:T(8,128)} %copy-done) | copy-start | bytes 8391172
  1384.1 486.8 %copy-start.11 = (f32[3642]{0:T(1024)S(1)}, f32[3642]{0:T(1024)}, u32[]{:S(2)}) copy-start(f32[3642]{0:T(1024)} %copy-done.10) | copy-start | bytes 43708
  1384.1 486.8 %copy-start.14 = (f32[3642]{0:T(1024)S(1)}, f32[3642]{0:T(1024)}, u32[]{:S(2)}) copy-start(f32[3642]{0:T(1024)} %copy-done.13) | copy-start | bytes 43708
  1384.1 486.8 %copy-start.21 = (f32[3642]{0:T(1024)S(1)}, f32[3642]{0:T(1024)}, u32[]{:S(2)}) copy-start(f32[3642]{0:T(1024)} %copy-done.20) | copy-start | bytes 43708
  1384.1 486.8 %copy-start.23 = (f32[3642]{0:T(1024)S(1)}, f32[3642]{0:T(1024)}, u32[]{:S(2)}) copy-start(f32[3642]{0:T(1024)} %copy-done.22) | copy-start | bytes 43708
  1384.2 486.8 %copy-start.25 = (f32[192]{0:T(256)S(1)}, f32[192]{0:T(256)}, u32[]{:S(2)}) copy-start(f32[192]{0:T(256)} %copy-done.24) | copy-start | bytes 2308
  1384.2 524.9 %reduce-scatter.59.cloned.1.call-start = ((), (), s32[]{:S(2)}) async-start(), calls=%async_computation.33 | async-start | bytes 40960
  1508.3 406.7 %reduce-scatter.57.cloned.1.call-start = ((), (), s32[]{:S(2)}) async-start(), calls=%async_computation.32 | async-start | bytes 40960
  1514.2 410.3 %all-reduce.6.cloned.1.call-start = ((), (), s32[]{:S(2)}) async-start(), calls=%async_computation.36 | async-start | bytes 3637248 | tf_op jit(solution)/shard_map/psum | solution.py:301
  1877.6 5.0 copy-start.7
Sparse Core Ops, SparseCore 0:
  85.2 104.1 all-gather.12
  312.2 191.0 reduce-scatter.32
  1312.0 190.8 reduce-scatter.38
  1505.8 20.5 reduce-scatter.54
  1529.2 19.6 reduce-scatter.52
  1551.2 19.5 reduce-scatter.62
  1573.1 19.5 reduce-scatter.60
  1595.7 19.5 reduce-scatter.50
  1618.2 19.5 reduce-scatter.48
  1640.2 32.8 reduce-scatter.46
  1676.2 32.8 reduce-scatter.44
  1711.9 22.0 reduce-scatter.42
  1736.6 30.3 reduce-scatter.40
  1769.2 101.7 reduce-scatter.34
  1873.2 19.8 reduce-scatter.58
  1895.4 19.5 reduce-scatter.56
Sparse Core Ops, SparseCore 1:
  314.7 15.6 all-gather.16
  542.6 186.5 all-gather.14
  731.2 15.7 all-gather.18
  827.4 192.0 reduce-scatter.36
  1767.1 56.7 all-reduce.5
